TPU v7x, 32 devices: a whole 2x2x4 slice. The times are simulated.
32 devices in a mesh: seq: 8 (over y, x, core), dp: 4 (over z).
Axes of the slice: x: 2, y: 2, z: 4, core: 2. Of those that a mesh axis runs over, the one named last changes fastest.
Arguments:
- layer_input: bfloat16 [4, 1024, 5120], P('dp', 'seq'), may hold values from -64 to 64, as said below
- out_grad: bfloat16 [4, 1024, 5120], P('dp', 'seq'), may hold values from -0.059814453 to 0.059814453
- w_query: bfloat16 [5120, 640], replicated, may hold values from -0.078125 to 0.078125
- w_key: bfloat16 [5120, 128], replicated, may hold values from -0.078125 to 0.078125
- w_value: bfloat16 [5120, 128], replicated, may hold values from -0.078125 to 0.078125
- w_output: bfloat16 [640, 5120], replicated, may hold values from -0.25 to 0.25
- block_mask: int32 [4, 8, 8], P('dp'), may hold values from 0 to 1, as said below
Outputs:
- grad_qkv: float32 [5120, 896], P(('seq', 'dp'))
- grad_output: float32 [640, 5120], P(('seq', 'dp'))
Inputs may be any that keep to these rules, and one draw needn't show every extreme that they name: `layer_input`: each position's entries are a bell-shaped or uniform body times a scale of that position; they may share a common direction, and some positions may repeat one strong vector. block_mask[r] has ones on its diagonal and zeros above it. The 8 blocks of sequence r form a shared prefix of at least half of them followed by a chosen branch and then a rejected branch, each of one block or more; a block attends every earlier or equal block of the prefix and of its own branch, and nothing else.
All inputs are finite; a program needn't handle non-finite values.
Results may differ from a plain program's by a relative error of at most 0.025.
The roundings to bfloat16 on the way count: a program that leaves them out, or rounds other values in their place, can miss the bound.
Values may be sent and summed in bfloat16 or wider, within the bound.
A program may use at most 128 MiB of HBM per device.

v0:
```python
import math
import jax
import jax.numpy as jnp
from jax import lax
from jax.sharding import PartitionSpec as P

BLOCK = 128


def allowed_block(mask_table, first_row, row_count, length):
    query_pos = first_row + jnp.arange(row_count, dtype=jnp.int32)
    key_pos = jnp.arange(length, dtype=jnp.int32)
    mask_rows = lax.dynamic_slice_in_dim(mask_table, first_row // BLOCK, row_count // BLOCK, 0)
    token_mask = jnp.repeat(jnp.repeat(mask_rows, BLOCK, axis=0), BLOCK, axis=1)
    same_block = query_pos[:, None] // BLOCK == key_pos[None, :] // BLOCK
    return (token_mask == 1) & (
        jnp.logical_not(same_block) | (key_pos[None, :] <= query_pos[:, None])
    )


def shards(layer_input, out_grad, w_query, w_key, w_value, w_output, block_mask):
    inputs_row = layer_input[0]
    grad_row = out_grad[0]
    mask_table = block_mask[0]
    tokens = inputs_row.shape[0]
    head_size = w_key.shape[1]
    group_heads = w_query.shape[1] // head_size
    scale = 1.0 / math.sqrt(head_size)
    queries = (
        jnp.dot(inputs_row, w_query, preferred_element_type=jnp.float32)
        .astype(jnp.bfloat16)
        .reshape(tokens, group_heads, head_size)
    )
    w_pair = jnp.concatenate([w_key, w_value], axis=1)
    kv_local = jnp.dot(inputs_row, w_pair, preferred_element_type=jnp.float32).astype(jnp.bfloat16)
    kv_all = lax.all_gather(kv_local, "seq", axis=0, tiled=True)
    length = kv_all.shape[0]
    key_rows = kv_all[:, :head_size]
    value_rows = kv_all[:, head_size:]
    first_row = lax.axis_index("seq") * tokens
    allowed = allowed_block(mask_table, first_row, tokens, length)
    attn_grad = (
        lax.dot_general(
            grad_row, w_output, (((1,), (1,)), ((), ())), preferred_element_type=jnp.float32
        )
        .astype(jnp.bfloat16)
        .reshape(tokens, group_heads, head_size)
    )
    scores = (
        jnp.einsum("tgh,sh->gts", queries, key_rows, preferred_element_type=jnp.float32) * scale
    )
    masked = jnp.where(allowed[None], scores, -jnp.inf)
    row_max = jnp.max(masked, axis=-1, keepdims=True)
    log_total = row_max + jnp.log(jnp.sum(jnp.exp(masked - row_max), axis=-1, keepdims=True))
    softmax_w = jnp.exp(masked - log_total)
    weights_b = softmax_w.astype(jnp.bfloat16)
    attn_out = jnp.einsum(
        "gts,sh->tgh", weights_b, value_rows, preferred_element_type=jnp.float32
    ).astype(jnp.bfloat16)
    row_delta = jnp.einsum(
        "tgh,tgh->gt", attn_grad.astype(jnp.float32), attn_out.astype(jnp.float32)
    )
    prob_grad = jnp.einsum("tgh,sh->gts", attn_grad, value_rows, preferred_element_type=jnp.float32)
    score_grad = (softmax_w * (prob_grad - row_delta[..., None])).astype(jnp.bfloat16)
    query_grad = (
        jnp.einsum("gts,sh->tgh", score_grad, key_rows, preferred_element_type=jnp.float32) * scale
    ).astype(jnp.bfloat16)
    query_grad = query_grad.reshape(tokens, group_heads * head_size)
    key_term = (
        jnp.einsum("gts,tgh->sh", score_grad, queries, preferred_element_type=jnp.float32) * scale
    )
    value_term = jnp.einsum("gts,tgh->sh", weights_b, attn_grad, preferred_element_type=jnp.float32)
    kv_grads = lax.psum_scatter(
        jnp.concatenate([key_term, value_term], axis=1), "seq", scatter_dimension=0, tiled=True
    )
    grads_all = jnp.concatenate([query_grad, kv_grads.astype(jnp.bfloat16)], axis=1)
    attn_flat = attn_out.reshape(tokens, group_heads * head_size)
    contract_rows = (((0,), (0,)), ((), ()))
    inputs_cols, grad_cols = (
        lax.all_to_all(inputs_row, "seq", split_axis=1, concat_axis=0, tiled=True),
        lax.all_to_all(grad_row, "seq", split_axis=1, concat_axis=0, tiled=True),
    )
    grads_seq, attn_seq = (
        lax.all_gather(grads_all, "seq", axis=0, tiled=True),
        lax.all_gather(attn_flat, "seq", axis=0, tiled=True),
    )
    qkv_cols = lax.dot_general(
        inputs_cols, grads_seq, contract_rows, preferred_element_type=jnp.float32
    )
    out_cols = lax.dot_general(
        attn_seq, grad_cols, contract_rows, preferred_element_type=jnp.float32
    )
    out_heads = lax.all_to_all(out_cols, "seq", split_axis=0, concat_axis=1, tiled=True)
    qkv_grad, output_grad = (
        lax.psum_scatter(qkv_cols, "dp", scatter_dimension=0, tiled=True),
        lax.psum_scatter(out_heads, "dp", scatter_dimension=0, tiled=True),
    )
    return (qkv_grad, output_grad)


def solution(mesh):
    placed = (P("dp", "seq", None), P("dp", "seq", None), P(), P(), P(), P(), P("dp", None, None))
    return jax.shard_map(
        shards,
        mesh=mesh,
        in_specs=placed,
        out_specs=(P(("seq", "dp"), None), P(("seq", "dp"), None)),
        check_vma=False,
    )
```

profile of v0, /device:TPU:0, one launch (start us, length us, event | category | flops | bytes accessed | tf_op | source)
XLA Modules:
  0.0 234.5 jit_solution(2066719553764132672)
XLA Ops:
  7.3 5.5 %fusion.18 = bf16[128,640]{1,0:T(8,128)(2,1)S(1)} fusion(bf16[640,5120]{1,0:T(8,128)(2,1)} %param.12, bf16[1,128,5120]{2,1,0:T(8,128)(2,1)} %param.8), kind=kOutput, calls=%fused_computation.23 | convolution fusion | flops 838942720 | bytes 8028160 | tf_op jit(solution)/shard_map/dot_general | solution.py:43
  12.9 4.2 %fusion.15 = bf16[128,640]{1,0:T(8,128)(2,1)S(1)} fusion(bf16[5120,640]{1,0:T(8,128)(2,1)} %param.9, bf16[1,128,5120]{2,1,0:T(8,128)(2,1)S(1)} %copy-done), kind=kOutput, calls=%fused_computation.22 | convolution fusion | flops 838942720 | bytes 8028160 | tf_op jit(solution)/shard_map/dot_general | solution.py:30
  17.3 2.2 fusion.26
  19.5 11.4 %all_gather.9 = bf16[1024,256]{0,1:T(8,128)(2,1)S(1)} all-gather(bf16[128,256]{0,1:T(8,128)(2,1)S(1)} %fusion.26), channel_id=1, replica_groups=mesh['seq'=8,'dp'=4] {'seq'}, dimensions={0}, use_global_device_ids=true | all-gather | bytes 589824 | tf_op jit(solution)/shard_map/all_gather | solution.py:36
  31.0 0.7 compare_bitcast_fusion
  32.1 0.6 fusion.40
  33.0 0.6 convolution_bitcast_fusion.1
  33.6 1.3 fusion.35
  34.9 0.7 fusion.6
  36.1 1.1 pad_maximum_fusion
  37.6 36.1 %reduce-scatter.7.cloned.1.call-done = f32[128,256]{0,1:T(8,128)} async-done(((f32[1024,256]{0,1:T(8,128)}), f32[128,256]{0,1:T(8,128)}) %reduce-scatter.7.cloned.1.call-update) | async-done | bytes 131088 | tf_op jit(solution)/shard_map/reduce_scatter | solution.py:73
  73.7 0.9 convert_element_type.45
  74.6 0.7 pad_maximum_fusion.1
  75.4 0.7 all-gather.5.cloned.1.call-update
  76.1 1.4 copy.53
  77.6 3.7 %all-to-all-start = ((bf16[128,8,640]{0,2,1:T(8,128)(2,1)}), bf16[128,8,640]{0,2,1:T(8,128)(2,1)S(1)}, u32[]{:S(2)}, u32[]{:S(2)}) async-start(bf16[128,8,640]{0,2,1:T(8,128)(2,1)} %bitcast.23), calls=%async_computation.1 | async-start | bytes 2621440 | tf_op jit(solution)/shard_map/all_to_all | solution.py:80
  81.5 1.2 copy.55
  82.7 19.2 %all-to-all-done = bf16[128,8,640]{0,2,1:T(8,128)(2,1)S(1)} async-done(((bf16[128,8,640]{0,2,1:T(8,128)(2,1)}), bf16[128,8,640]{0,2,1:T(8,128)(2,1)S(1)}, u32[]{:S(2)}, u32[]{:S(2)}) %all-to-all-start) | async-done | bytes 1310752 | tf_op jit(solution)/shard_map/all_to_all | solution.py:80
  101.9 4.3 %all-to-all-start.1 = ((bf16[128,8,640]{2,0,1:T(8,128)(2,1)}), bf16[128,8,640]{2,0,1:T(8,128)(2,1)}, u32[]{:S(2)}, u32[]{:S(2)}) async-start(bf16[128,8,640]{2,0,1:T(8,128)(2,1)} %copy.55), calls=%async_computation.2 | async-start | bytes 2621440 | tf_op jit(solution)/shard_map/all_to_all | solution.py:81
  106.2 1.4 copy.54
  107.6 1.0 all-gather.3.cloned.1.call-done
  108.7 3.5 %convolution_bitcast_fusion = f32[640,896]{0,1:T(8,128)S(1)} fusion(bf16[1024,896]{0,1:T(8,128)(2,1)} %all-gather.3.cloned.1.call-done, bf16[1024,640]{1,0:T(8,128)(2,1)} %bitcast.108), kind=kOutput, calls=%fused_computation.11 | convolution fusion | flops 1174405120 | bytes 5439488 | tf_op jit(solution)/shard_map/dot_general | solution.py:87
  112.1 2.1 copy.76
  114.2 11.9 %all-to-all-done.1 = bf16[128,8,640]{2,0,1:T(8,128)(2,1)} async-done(((bf16[128,8,640]{2,0,1:T(8,128)(2,1)}), bf16[128,8,640]{2,0,1:T(8,128)(2,1)}, u32[]{:S(2)}, u32[]{:S(2)}) %all-to-all-start.1) | async-done | bytes 1310752 | tf_op jit(solution)/shard_map/all_to_all | solution.py:81
  126.2 10.7 %all-gather.5.cloned.1.call-done = bf16[1024,640]{0,1:T(8,128)(2,1)} async-done(((bf16[128,640]{0,1:T(8,128)(2,1)}), bf16[1024,640]{0,1:T(8,128)(2,1)}) %all-gather.5.cloned.1.call-update) | async-done | bytes 1310736 | tf_op jit(solution)/shard_map/all_gather | solution.py:85
  136.8 2.9 %fusion.41 = f32[8,80,640]{2,1,0:T(8,128)S(1)} fusion(bf16[8,80,1024]{2,1,0:T(8,128)(2,1)} %bitcast.113, bf16[1024,640,1]{1,0,2:T(8,128)(2,1)} %bitcast.32), kind=kOutput, calls=%fused_computation.54 | convolution fusion | flops 838860800 | bytes 4259840 | tf_op jit(solution)/shard_map/dot_general | solution.py:90
  139.7 24.2 %all_to_all.54 = f32[8,80,640]{2,1,0:T(8,128)S(1)} all-to-all(f32[8,80,640]{2,1,0:T(8,128)S(1)} %fusion.41), channel_id=1, replica_groups=mesh['seq'=8,'dp'=4] {'seq'}, dimensions={0} | all-to-all | bytes 3276800 | tf_op jit(solution)/shard_map/all_to_all | solution.py:93
  164.1 54.3 %fusion = f32[24,5120]{1,0:T(8,128)S(1)} fusion(f32[80,5120]{1,0:T(8,128)S(1)} %bitcast.101), kind=kCustom, calls=%all-reduce-scatter | all-reduce-scatter fusion | flops 491521 | bytes 2130432
  218.4 1.3 collective-permute-start
  219.8 0.6 dynamic-slice.5
  221.0 5.6 %collective-permute-done = f32[12,5120]{1,0:T(8,128)S(1)} collective-permute-done((f32[12,5120]{1,0:T(8,128)S(1)}, f32[12,5120]{1,0:T(8,128)S(1)}, u32[]{:S(2)}, u32[]{:S(2)}) %collective-permute-start) | collective-permute-done | bytes 245792
  227.2 0.8 constant_dynamic-slice_fusion
  (30 shorter events, 3.1 us)
Async XLA Ops:
  7.2 66.6 %reduce-scatter.7.cloned.1.call-start = ((), (), s32[]{:S(2)}) async-start(), calls=%async_computation.5 | async-start | bytes 1179648 | tf_op jit(solution)/shard_map/reduce_scatter | solution.py:73
  7.2 5.7 %copy-start = (bf16[1,128,5120]{2,1,0:T(8,128)(2,1)S(1)}, bf16[1,128,5120]{2,1,0:T(8,128)(2,1)}, u32[]{:S(2)}) copy-start(bf16[1,128,5120]{2,1,0:T(8,128)(2,1)} %param.7) | copy-start | bytes 3932164
  12.9 4.3 %copy-start.3 = (bf16[5120,128]{1,0:T(8,128)(2,1)S(1)}, bf16[5120,128]{1,0:T(8,128)(2,1)}, u32[]{:S(2)}) copy-start(bf16[5120,128]{1,0:T(8,128)(2,1)} %param.11) | copy-start | bytes 3932164
  37.2 71.4 %all-gather.3.cloned.1.call-start = ((), (), s32[]{:S(2)}) async-start(), calls=%async_computation.6 | async-start | bytes 2064384 | tf_op jit(solution)/shard_map/all_gather | solution.py:84
  75.4 61.5 %all-gather.5.cloned.1.call-start = ((), (), s32[]{:S(2)}) async-start(), calls=%async_computation.7 | async-start | bytes 1474560 | tf_op jit(solution)/shard_map/all_gather | solution.py:85
  77.6 3.7 %copy-start.1 = (bf16[1,128,5120]{2,1,0:T(8,128)(2,1)S(1)}, bf16[1,128,5120]{2,1,0:T(8,128)(2,1)}, u32[]{:S(2)}) copy-start(bf16[1,128,5120]{2,1,0:T(8,128)(2,1)} %param.8) | copy-start | bytes 3932164
  77.6 24.3 %all-to-all-start = ((bf16[128,8,640]{0,2,1:T(8,128)(2,1)}), bf16[128,8,640]{0,2,1:T(8,128)(2,1)S(1)}, u32[]{:S(2)}, u32[]{:S(2)}) async-start(bf16[128,8,640]{0,2,1:T(8,128)(2,1)} %bitcast.23), calls=%async_computation.1 | async-start | bytes 2621440 | tf_op jit(solution)/shard_map/all_to_all | solution.py:80
  101.9 24.3 %all-to-all-start.1 = ((bf16[128,8,640]{2,0,1:T(8,128)(2,1)}), bf16[128,8,640]{2,0,1:T(8,128)(2,1)}, u32[]{:S(2)}, u32[]{:S(2)}) async-start(bf16[128,8,640]{2,0,1:T(8,128)(2,1)} %copy.55), calls=%async_computation.2 | async-start | bytes 2621440 | tf_op jit(solution)/shard_map/all_to_all | solution.py:81
  106.2 121.8 %reduce-scatter.9.cloned.1.call-start = ((), (), s32[]{:S(2)}) async-start(), calls=%async_computation.8 | async-start | bytes 2867200
  164.1 55.7 %copy-start.2 = (u32[32]{0:T(128)S(1)}, u32[32]{0:T(128)}, u32[]{:S(2)}) copy-start(u32[32]{0:T(128)} %constant.62) | copy-start | bytes 388
  218.4 8.2 %collective-permute-start = (f32[12,5120]{1,0:T(8,128)S(1)}, f32[12,5120]{1,0:T(8,128)S(1)}, u32[]{:S(2)}, u32[]{:S(2)}) collective-permute-start(f32[12,5120]{1,0:T(8,128)S(1)} %slice.10), channel_id=1, source_target_pairs={{0,1},{1,2},{2,3},{4,5},{5,6},{6,7},{8,9},{9,10},{10,11},{12,13},{... | collective-permute-start | bytes 737288
Sparse Core Ops, SparseCore 0:
  37.3 36.3 reduce-scatter.6
  76.2 32.4 all-gather.2
  110.5 26.2 all-gather.4
  139.6 58.8 reduce-scatter.8
where the time goes:
time: 235 us
  blocking collectives  90 us (38%)
  waiting for transfers between devices  85.2 us (36%)
  matrix products  22.2 us (9%)
  between operations  14.6 us (6%)
  starting transfers between devices  9.44 us (4%)
  local copies, waits for them, and re-layouts  8.93 us (4%)
  other arithmetic  4.09 us (2%)
    unnamed x1, blocking collectives  54.3 us
    reduce_scatter x1, waiting for transfers between devices, shards(): lax.psum_scatter(jnp.concatenate([key_term, value_term], axis=1), 'seq',...  36.1 us
    all_to_all x1, blocking collectives, shards(): lax.all_to_all(out_cols, 'seq', split_axis=0, concat_axis=1, tiled=True)  24.2 us
    all_to_all x1, waiting for transfers between devices, shards(): lax.all_to_all(inputs_row, 'seq', split_axis=1, concat_axis=0, tiled=True)  19.2 us
    all_to_all x1, waiting for transfers between devices, shards(): lax.all_to_all(grad_row, 'seq', split_axis=1, concat_axis=0, tiled=True)  11.9 us
    all_gather x1, blocking collectives, shards(): kv_all = lax.all_gather(kv_local, 'seq', axis=0, tiled=True)  11.4 us
    all_gather x1, waiting for transfers between devices, shards(): lax.all_gather(attn_flat, 'seq', axis=0, tiled=True)  10.7 us
    unnamed x6, waiting for transfers between devices  6.38 us
  transfers between devices with their start and end apart: 7, of which 6 were waited for; matrix products, arithmetic and copies ran while one was open for 30% of the time, Pallas kernels for 0%

commit v1 on v0

--- a/solution.py
+++ b/solution.py
@@ -33,7 +33,12 @@
     )
     w_pair = jnp.concatenate([w_key, w_value], axis=1)
     kv_local = jnp.dot(inputs_row, w_pair, preferred_element_type=jnp.float32).astype(jnp.bfloat16)
-    kv_all = lax.all_gather(kv_local, "seq", axis=0, tiled=True)
+    ring = [kv_local]
+    for hop in range(7):
+        ring.append(lax.ppermute(ring[-1], "seq", [(dev, (dev + 1) % 8) for dev in range(8)]))
+    kv_all = jnp.roll(
+        jnp.concatenate(ring[::-1], axis=0), (lax.axis_index("seq") + 1) * ring[0].shape[0], axis=0
+    )
     length = kv_all.shape[0]
     key_rows = kv_all[:, :head_size]
     value_rows = kv_all[:, head_size:]

time: 235 us -> 247 us (1.051)
  waiting for transfers between devices: 85.2 us -> 106 us
  blocking collectives: 90 us -> 78.9 us
    ppermute x0 -> x7, waiting for transfers between devices: none -> 22.5 us  [shards(): lax.ppermute(ring[-1], 'seq', [(dev, (dev + 1) % 8) for dev in range(8)])]
    all_gather x1 -> x0, blocking collectives: 11.4 us -> none  [shards(): kv_all = lax.all_gather(kv_local, 'seq', axis=0, tiled=True)]
    dot_general x1, matrix products: 5.48 us -> 2.14 us  [shards(): lax.dot_general(grad_row, w_output, (((1,), (1,)), ((), ())), preferred_e...]
    all_to_all x1, waiting for transfers between devices: 11.9 us -> 8.65 us  [shards(): lax.all_to_all(grad_row, 'seq', split_axis=1, concat_axis=0, tiled=True)]
    unnamed x15 -> x36, local copies, waits for them, and re-layouts: 5.74 us -> 6.93 us
  transfers between devices with their start and end apart: 7 -> 14, of which waited for: 6 -> 13; matrix products, arithmetic and copies ran while one was open for 30% -> 33% of each run, Pallas kernels for 0% -> 0%
where the time goes in v1:
time: 247 us; the launch traced here: 246 us
  waiting for transfers between devices  106 us (43%)
  blocking collectives  78.9 us (32%)
  matrix products  21.5 us (9%)
  between operations  14.8 us (6%)
  starting transfers between devices  11.1 us (4%)
  local copies, waits for them, and re-layouts  10.2 us (4%)
  other arithmetic  4.12 us (2%)
    unnamed x1, blocking collectives  54.7 us
    reduce_scatter x1, waiting for transfers between devices, shards(): lax.psum_scatter(jnp.concatenate([key_term, value_term], axis=1), 'seq',...  35.8 us
    all_to_all x1, blocking collectives, shards(): lax.all_to_all(out_cols, 'seq', split_axis=0, concat_axis=1, tiled=True)  24.2 us
    ppermute x7, waiting for transfers between devices, shards(): lax.ppermute(ring[-1], 'seq', [(dev, (dev + 1) % 8) for dev in range(8)])  22.5 us
    all_to_all x1, waiting for transfers between devices, shards(): lax.all_to_all(inputs_row, 'seq', split_axis=1, concat_axis=0, tiled=True)  19.2 us
    all_gather x1, waiting for transfers between devices, shards(): lax.all_gather(attn_flat, 'seq', axis=0, tiled=True)  11.4 us
    all_to_all x1, waiting for transfers between devices, shards(): lax.all_to_all(grad_row, 'seq', split_axis=1, concat_axis=0, tiled=True)  8.65 us
    unnamed x36, local copies, waits for them, and re-layouts  6.93 us
  transfers between devices with their start and end apart: 14, of which 13 were waited for; matrix products, arithmetic and copies ran while one was open for 33% of the time, Pallas kernels for 0%

profile of v1, /device:TPU:0, one launch (start us, length us, event | category | flops | bytes accessed | tf_op | source)
XLA Modules:
  0.0 246.2 jit_solution(14328379050083052800)
XLA Ops:
  7.2 2.8 %fusion.26 = bf16[128,256]{1,0:T(8,128)(2,1)S(1)} fusion(bf16[5120,128]{1,0:T(8,128)(2,1)} %param.11, bf16[5120,128]{1,0:T(8,128)(2,1)} %param.10, bf16[1,128,5120]{2,1,0:T(8,128)(2,1)} %param.7), kind=kOutput, calls=%fused_computation.26 | convolution fusion | flops 340819968 | bytes 3997696 | tf_op jit(solution)/shard_map/dot_general | solution.py:35
  10.5 4.3 %fusion.15 = bf16[128,640]{1,0:T(8,128)(2,1)S(1)} fusion(bf16[5120,640]{1,0:T(8,128)(2,1)} %param.9, bf16[1,128,5120]{2,1,0:T(8,128)(2,1)S(1)} %copy-done), kind=kOutput, calls=%fused_computation.22 | convolution fusion | flops 838942720 | bytes 8028160 | tf_op jit(solution)/shard_map/dot_general | solution.py:30
  15.4 1.9 collective-permute-start.1
  17.3 2.1 fusion.18
  20.7 3.9 %collective-permute-done.2 = bf16[128,256]{1,0:T(8,128)(2,1)S(1)} collective-permute-done((bf16[128,256]{1,0:T(8,128)(2,1)S(1)}, bf16[128,256]{1,0:T(8,128)(2,1)S(1)}, u32[]{:S(2)}, u32[]{:S(2)}) %collective-permute-start.2) | collective-permute-done | bytes 65568 | tf_op jit(solution)/shard_map/ppermute | solution.py:38
  24.6 4.5 %collective-permute-done.3 = bf16[128,256]{1,0:T(8,128)(2,1)S(1)} collective-permute-done((bf16[128,256]{1,0:T(8,128)(2,1)S(1)}, bf16[128,256]{1,0:T(8,128)(2,1)S(1)}, u32[]{:S(2)}, u32[]{:S(2)}) %collective-permute-start.3) | collective-permute-done | bytes 65568 | tf_op jit(solution)/shard_map/ppermute | solution.py:38
  29.1 4.6 %collective-permute-done.4 = bf16[128,256]{1,0:T(8,128)(2,1)S(1)} collective-permute-done((bf16[128,256]{1,0:T(8,128)(2,1)S(1)}, bf16[128,256]{1,0:T(8,128)(2,1)S(1)}, u32[]{:S(2)}, u32[]{:S(2)}) %collective-permute-start.4) | collective-permute-done | bytes 65568 | tf_op jit(solution)/shard_map/ppermute | solution.py:38
  33.7 4.6 %collective-permute-done.5 = bf16[128,256]{1,0:T(8,128)(2,1)S(1)} collective-permute-done((bf16[128,256]{1,0:T(8,128)(2,1)S(1)}, bf16[128,256]{1,0:T(8,128)(2,1)S(1)}, u32[]{:S(2)}, u32[]{:S(2)}) %collective-permute-start.5) | collective-permute-done | bytes 65568 | tf_op jit(solution)/shard_map/ppermute | solution.py:38
  39.0 3.9 %collective-permute-done.6 = bf16[128,256]{1,0:T(8,128)(2,1)S(1)} collective-permute-done((bf16[128,256]{1,0:T(8,128)(2,1)S(1)}, bf16[128,256]{1,0:T(8,128)(2,1)S(1)}, u32[]{:S(2)}, u32[]{:S(2)}) %collective-permute-start.6) | collective-permute-done | bytes 65568 | tf_op jit(solution)/shard_map/ppermute | solution.py:38
  44.6 1.3 fusion.35
  47.1 1.1 pad_maximum_fusion
  48.3 1.4 fusion.14
  49.7 35.8 %reduce-scatter.7.cloned.1.call-done = f32[128,256]{0,1:T(8,128)} async-done(((f32[1024,256]{0,1:T(8,128)}), f32[128,256]{0,1:T(8,128)}) %reduce-scatter.7.cloned.1.call-update) | async-done | bytes 131088 | tf_op jit(solution)/shard_map/reduce_scatter | solution.py:78
  85.5 0.9 convert_element_type.45
  86.4 0.7 pad_maximum_fusion.1
  87.9 1.4 copy.53
  89.3 3.7 %all-to-all-start = ((bf16[128,8,640]{0,2,1:T(8,128)(2,1)}), bf16[128,8,640]{0,2,1:T(8,128)(2,1)S(1)}, u32[]{:S(2)}, u32[]{:S(2)}) async-start(bf16[128,8,640]{0,2,1:T(8,128)(2,1)} %bitcast.23), calls=%async_computation.1 | async-start | bytes 2621440 | tf_op jit(solution)/shard_map/all_to_all | solution.py:85
  93.3 1.2 copy.55
  94.5 19.2 %all-to-all-done = bf16[128,8,640]{0,2,1:T(8,128)(2,1)S(1)} async-done(((bf16[128,8,640]{0,2,1:T(8,128)(2,1)}), bf16[128,8,640]{0,2,1:T(8,128)(2,1)S(1)}, u32[]{:S(2)}, u32[]{:S(2)}) %all-to-all-start) | async-done | bytes 1310752 | tf_op jit(solution)/shard_map/all_to_all | solution.py:85
  113.7 3.6 %all-to-all-start.1 = ((bf16[128,8,640]{2,0,1:T(8,128)(2,1)}), bf16[128,8,640]{2,0,1:T(8,128)(2,1)S(1)}, u32[]{:S(2)}, u32[]{:S(2)}) async-start(bf16[128,8,640]{2,0,1:T(8,128)(2,1)} %copy.55), calls=%async_computation.2 | async-start | bytes 2621440 | tf_op jit(solution)/shard_map/all_to_all | solution.py:86
  117.3 1.5 copy.54
  118.8 1.6 all-gather.3.cloned.1.call-done
  120.4 4.8 %convolution_bitcast_fusion = f32[640,896]{0,1:T(8,128)} fusion(bf16[1024,896]{0,1:T(8,128)(2,1)} %all-gather.3.cloned.1.call-done, bf16[1024,640]{1,0:T(8,128)(2,1)} %bitcast.113), kind=kOutput, calls=%fused_computation.11 | convolution fusion | flops 1174405120 | bytes 5439488 | tf_op jit(solution)/shard_map/dot_general | solution.py:92
  125.3 3.2 %copy.76 = f32[640,896]{1,0:T(8,128)} copy(f32[640,896]{0,1:T(8,128)} %convolution_bitcast_fusion) | data formatting | bytes 4587520
  128.5 8.6 %all-to-all-done.1 = bf16[128,8,640]{2,0,1:T(8,128)(2,1)S(1)} async-done(((bf16[128,8,640]{2,0,1:T(8,128)(2,1)}), bf16[128,8,640]{2,0,1:T(8,128)(2,1)S(1)}, u32[]{:S(2)}, u32[]{:S(2)}) %all-to-all-start.1) | async-done | bytes 1310752 | tf_op jit(solution)/shard_map/all_to_all | solution.py:86
  137.1 11.4 %all-gather.5.cloned.1.call-done = bf16[1024,640]{0,1:T(8,128)(2,1)} async-done(((bf16[128,640]{0,1:T(8,128)(2,1)}), bf16[1024,640]{0,1:T(8,128)(2,1)}) %all-gather.5.cloned.1.call-update) | async-done | bytes 1310736 | tf_op jit(solution)/shard_map/all_gather | solution.py:90
  148.5 2.5 %fusion.43 = f32[8,80,640]{2,1,0:T(8,128)S(1)} fusion(bf16[8,80,1024]{2,1,0:T(8,128)(2,1)} %bitcast.116, bf16[1024,640,1]{1,0,2:T(8,128)(2,1)S(1)} %bitcast.112), kind=kOutput, calls=%fused_computation.72 | convolution fusion | flops 838860800 | bytes 4259840 | tf_op jit(solution)/shard_map/dot_general | solution.py:95
  151.0 24.2 %all_to_all.54 = f32[8,80,640]{2,1,0:T(8,128)S(1)} all-to-all(f32[8,80,640]{2,1,0:T(8,128)S(1)} %fusion.43), channel_id=1, replica_groups=mesh['seq'=8,'dp'=4] {'seq'}, dimensions={0} | all-to-all | bytes 3276800 | tf_op jit(solution)/shard_map/all_to_all | solution.py:98
  175.4 54.7 %fusion = f32[24,5120]{1,0:T(8,128)S(1)} fusion(f32[80,5120]{1,0:T(8,128)S(1)} %bitcast.101), kind=kCustom, calls=%all-reduce-scatter | all-reduce-scatter fusion | flops 491521 | bytes 2130432
  230.1 1.3 collective-permute-start.7
  232.7 5.7 %collective-permute-done.7 = f32[12,5120]{1,0:T(8,128)S(1)} collective-permute-done((f32[12,5120]{1,0:T(8,128)S(1)}, f32[12,5120]{1,0:T(8,128)S(1)}, u32[]{:S(2)}, u32[]{:S(2)}) %collective-permute-start.7) | collective-permute-done | bytes 245792
  238.9 0.8 constant_dynamic-slice_fusion
  (66 shorter events, 8.2 us)
Async XLA Ops:
  7.2 3.4 %copy-start = (bf16[1,128,5120]{2,1,0:T(8,128)(2,1)S(1)}, bf16[1,128,5120]{2,1,0:T(8,128)(2,1)}, u32[]{:S(2)}) copy-start(bf16[1,128,5120]{2,1,0:T(8,128)(2,1)} %param.7) | copy-start | bytes 3932164
  7.2 78.3 %reduce-scatter.7.cloned.1.call-start = ((), (), s32[]{:S(2)}) async-start(), calls=%async_computation.5 | async-start | bytes 1179648 | tf_op jit(solution)/shard_map/reduce_scatter | solution.py:78
  7.2 10.0 %slice-start = ((s8[6553600]{0:T(1024)(128)(4,1)}), s8[4194304]{0:T(1024)(128)(4,1)S(1)}, s32[]{:S(2)}) async-start(s8[6553600]{0:T(1024)(128)(4,1)} %bitcast.102), calls=%async_computation.9 | async-start | bytes 8388608
  10.0 7.3 %slice-start.1 = ((s8[6553600]{0:T(1024)(128)(4,1)}), s8[2359296]{0:T(1024)(128)(4,1)S(1)}, s32[]{:S(2)}) async-start(s8[6553600]{0:T(1024)(128)(4,1)} %bitcast.102), calls=%async_computation.10 | async-start | bytes 4718592
  10.0 7.2 %copy-start.1 = (bf16[1,128,5120]{2,1,0:T(8,128)(2,1)S(1)}, bf16[1,128,5120]{2,1,0:T(8,128)(2,1)}, u32[]{:S(2)}) copy-start(bf16[1,128,5120]{2,1,0:T(8,128)(2,1)} %param.8) | copy-start | bytes 3932164
  10.0 5.3 %collective-permute-start = (bf16[128,256]{1,0:T(8,128)(2,1)S(1)}, bf16[128,256]{1,0:T(8,128)(2,1)S(1)}, u32[]{:S(2)}, u32[]{:S(2)}) collective-permute-start(bf16[128,256]{1,0:T(8,128)(2,1)S(1)} %fusion.26), channel_id=1, source_target_pairs={{0,4},{4,8},{8,12},{12,16},{16,20},{20,24},{24,28},{28,0},{1,5},{5... | collective-permute-start | bytes 196616 | tf_op jit(solution)/shard_map/ppermute | solution.py:38
  15.4 4.6 %collective-permute-start.1 = (bf16[128,256]{1,0:T(8,128)(2,1)S(1)}, bf16[128,256]{1,0:T(8,128)(2,1)S(1)}, u32[]{:S(2)}, u32[]{:S(2)}) collective-permute-start(bf16[128,256]{1,0:T(8,128)(2,1)S(1)} %collective-permute-done), channel_id=1, source_target_pairs={{0,4},{4,8},{8,12},{12,16},{16,20},{20,24},{24,28},{28,0},{1,5},{5... | collective-permute-start | bytes 196616 | tf_op jit(solution)/shard_map/ppermute | solution.py:38
  20.0 4.6 %collective-permute-start.2 = (bf16[128,256]{1,0:T(8,128)(2,1)S(1)}, bf16[128,256]{1,0:T(8,128)(2,1)S(1)}, u32[]{:S(2)}, u32[]{:S(2)}) collective-permute-start(bf16[128,256]{1,0:T(8,128)(2,1)S(1)} %collective-permute-done.1), channel_id=1, source_target_pairs={{0,4},{4,8},{8,12},{12,16},{16,20},{20,24},{24,28},{28,0},{1,5},{5... | collective-permute-start | bytes 196616 | tf_op jit(solution)/shard_map/ppermute | solution.py:38
  24.5 4.6 %collective-permute-start.3 = (bf16[128,256]{1,0:T(8,128)(2,1)S(1)}, bf16[128,256]{1,0:T(8,128)(2,1)S(1)}, u32[]{:S(2)}, u32[]{:S(2)}) collective-permute-start(bf16[128,256]{1,0:T(8,128)(2,1)S(1)} %collective-permute-done.2), channel_id=1, source_target_pairs={{0,4},{4,8},{8,12},{12,16},{16,20},{20,24},{24,28},{28,0},{1,5},{5... | collective-permute-start | bytes 196616 | tf_op jit(solution)/shard_map/ppermute | solution.py:38
  29.1 4.6 %collective-permute-start.4 = (bf16[128,256]{1,0:T(8,128)(2,1)S(1)}, bf16[128,256]{1,0:T(8,128)(2,1)S(1)}, u32[]{:S(2)}, u32[]{:S(2)}) collective-permute-start(bf16[128,256]{1,0:T(8,128)(2,1)S(1)} %collective-permute-done.3), channel_id=1, source_target_pairs={{0,4},{4,8},{8,12},{12,16},{16,20},{20,24},{24,28},{28,0},{1,5},{5... | collective-permute-start | bytes 196616 | tf_op jit(solution)/shard_map/ppermute | solution.py:38
  33.7 4.6 %collective-permute-start.5 = (bf16[128,256]{1,0:T(8,128)(2,1)S(1)}, bf16[128,256]{1,0:T(8,128)(2,1)S(1)}, u32[]{:S(2)}, u32[]{:S(2)}) collective-permute-start(bf16[128,256]{1,0:T(8,128)(2,1)S(1)} %collective-permute-done.4), channel_id=1, source_target_pairs={{0,4},{4,8},{8,12},{12,16},{16,20},{20,24},{24,28},{28,0},{1,5},{5... | collective-permute-start | bytes 196616 | tf_op jit(solution)/shard_map/ppermute | solution.py:38
  38.3 4.6 %collective-permute-start.6 = (bf16[128,256]{1,0:T(8,128)(2,1)S(1)}, bf16[128,256]{1,0:T(8,128)(2,1)S(1)}, u32[]{:S(2)}, u32[]{:S(2)}) collective-permute-start(bf16[128,256]{1,0:T(8,128)(2,1)S(1)} %collective-permute-done.5), channel_id=1, source_target_pairs={{0,4},{4,8},{8,12},{12,16},{16,20},{20,24},{24,28},{28,0},{1,5},{5... | collective-permute-start | bytes 196616 | tf_op jit(solution)/shard_map/ppermute | solution.py:38
  43.1 2.8 %copy-start.3 = (bf16[2048,256]{1,0:T(8,128)(2,1)}, bf16[2048,256]{1,0:T(8,128)(2,1)S(1)}, u32[]{:S(2)}) copy-start(bf16[2048,256]{1,0:T(8,128)(2,1)S(1)} %constant_dynamic-update-slice_fusion) | copy-start | bytes 3145732
  48.3 72.2 %all-gather.3.cloned.1.call-start = ((), (), s32[]{:S(2)}) async-start(), calls=%async_computation.6 | async-start | bytes 2064384 | tf_op jit(solution)/shard_map/all_gather | solution.py:89
  87.1 61.4 %all-gather.5.cloned.1.call-start = ((), (), s32[]{:S(2)}) async-start(), calls=%async_computation.7 | async-start | bytes 1474560 | tf_op jit(solution)/shard_map/all_gather | solution.py:90
  89.3 3.7 %copy-start.2 = (bf16[1,128,5120]{2,1,0:T(8,128)(2,1)S(1)}, bf16[1,128,5120]{2,1,0:T(8,128)(2,1)}, u32[]{:S(2)}) copy-start(bf16[1,128,5120]{2,1,0:T(8,128)(2,1)} %param.8) | copy-start | bytes 3932164
  89.3 24.3 %all-to-all-start = ((bf16[128,8,640]{0,2,1:T(8,128)(2,1)}), bf16[128,8,640]{0,2,1:T(8,128)(2,1)S(1)}, u32[]{:S(2)}, u32[]{:S(2)}) async-start(bf16[128,8,640]{0,2,1:T(8,128)(2,1)} %bitcast.23), calls=%async_computation.1 | async-start | bytes 2621440 | tf_op jit(solution)/shard_map/all_to_all | solution.py:85
  113.7 23.5 %all-to-all-start.1 = ((bf16[128,8,640]{2,0,1:T(8,128)(2,1)}), bf16[128,8,640]{2,0,1:T(8,128)(2,1)S(1)}, u32[]{:S(2)}, u32[]{:S(2)}) async-start(bf16[128,8,640]{2,0,1:T(8,128)(2,1)} %copy.55), calls=%async_computation.2 | async-start | bytes 2621440 | tf_op jit(solution)/shard_map/all_to_all | solution.py:86
  117.2 122.4 %reduce-scatter.9.cloned.1.call-start = ((), (), s32[]{:S(2)}) async-start(), calls=%async_computation.8 | async-start | bytes 2867200
  175.4 56.1 %copy-start.4 = (u32[32]{0:T(128)S(1)}, u32[32]{0:T(128)}, u32[]{:S(2)}) copy-start(u32[32]{0:T(128)} %constant.84) | copy-start | bytes 388
  230.1 8.2 %collective-permute-start.7 = (f32[12,5120]{1,0:T(8,128)S(1)}, f32[12,5120]{1,0:T(8,128)S(1)}, u32[]{:S(2)}, u32[]{:S(2)}) collective-permute-start(f32[12,5120]{1,0:T(8,128)S(1)} %slice.8), channel_id=1, source_target_pairs={{0,1},{1,2},{2,3},{4,5},{5,6},{6,7},{8,9},{9,10},{10,11},{12,13},{... | collective-permute-start | bytes 737288
Sparse Core Ops, SparseCore 0:
  48.4 37.0 reduce-scatter.6
  88.0 32.4 all-gather.2
  122.3 26.1 all-gather.4
  151.3 59.2 reduce-scatter.8
